TPU v7x, 32 devices: a whole 2x2x4 slice. The times are simulated.
32 devices in a mesh: dp: 4 (over y, core), feat: 8 (over z, x).
Axes of the slice: x: 2, y: 2, z: 4, core: 2. Of those that a mesh axis runs over, the one named last changes fastest.
Arguments:
- images: bfloat16 [1536, 3072], P('dp'), may hold values from -6 to 6
- labels: int32 [1536], P('dp'), may hold values from 0 to 9
- frequencies: bfloat16 [3072, 8192], P(None, 'feat'), may hold values from -0.15625 to 0.15625
- privacy_noise: float32 [10, 2, 8192], P(None, None, 'feat'), may hold values from -0.6 to 0.6
- latents: bfloat16 [1024, 256], P('dp'), may hold values from -6 to 6
- gen_labels: int32 [1024], P('dp'), may hold values from 0 to 9
- gen_in: bfloat16 [256, 1024], replicated, may hold values from -0.375 to 0.375
- gen_out: bfloat16 [1024, 3072], replicated, may hold values from -0.25 to 0.25
Outputs:
- match_loss: float32 [], replicated
- grad_in: float32 [256, 1024], P('dp')
- grad_out: float32 [1024, 3072], P('dp')
All inputs are finite; a program needn't handle non-finite values.
Results may differ from a plain program's by a relative error of at most 0.0035.
Values sent between devices are 32-bit elements; how exact they have to be, the bound alone decides.
No kernel may reach another device: no remote copies, remote signals or barrier semaphores. Data moves between devices by JAX's collectives and lax.ppermute only.
A program may use at most 128 MiB of HBM per device.

v0:
```python
import jax
import jax.numpy as jnp
from jax import lax
from jax.sharding import PartitionSpec as P


def class_sums(phase, classes_of, classes, scale):
    feats = jnp.concatenate([jnp.cos(phase), jnp.sin(phase)], axis=1)
    onehot = (classes_of[:, None] == jnp.arange(classes)[None, :]).astype(jnp.float32)
    sums = jnp.dot(onehot.T, feats, precision=lax.Precision.HIGHEST) * scale
    return (sums.reshape(classes, 2, phase.shape[1]), onehot)


def generator_grads(image_grad, image_out, hidden, pre_hidden, sigmoid_h, latents, gen_out):
    out_grad = (image_grad * (1.0 - image_out * image_out)).astype(jnp.bfloat16)
    grad_out = jnp.einsum("gh,gd->hd", hidden, out_grad, preferred_element_type=jnp.float32)
    back_hidden = jnp.einsum("gd,hd->gh", out_grad, gen_out, preferred_element_type=jnp.float32)
    hidden_grad = (back_hidden * sigmoid_h * (1.0 + pre_hidden * (1.0 - sigmoid_h))).astype(
        jnp.bfloat16
    )
    grad_in = jnp.einsum("gz,gh->zh", latents, hidden_grad, preferred_element_type=jnp.float32)
    return (grad_in, grad_out)


def per_device(images, labels, frequencies, privacy_noise, latents, gen_labels, gen_in, gen_out):
    classes = privacy_noise.shape[0]
    feat_dev = frequencies.shape[1]
    data_devices = lax.axis_size("dp")
    feat_devices = lax.axis_size("feat")
    total_images = images.shape[0] * data_devices
    total_gen = latents.shape[0] * data_devices
    total_feats = feat_dev * feat_devices
    data_phase = jnp.dot(images, frequencies, preferred_element_type=jnp.float32)
    data_part, unused = class_sums(data_phase, labels, classes, classes / total_images)
    pre_hidden = jnp.dot(latents, gen_in, preferred_element_type=jnp.float32)
    sigmoid_h = jax.nn.sigmoid(pre_hidden)
    hidden = (pre_hidden * sigmoid_h).astype(jnp.bfloat16)
    image_out = jnp.tanh(jnp.dot(hidden, gen_out, preferred_element_type=jnp.float32))
    gen_image = image_out.astype(jnp.bfloat16)
    gen_phase = jnp.dot(gen_image, frequencies, preferred_element_type=jnp.float32)
    gen_part, gen_onehot = class_sums(gen_phase, gen_labels, classes, classes / total_gen)
    mean_gap = lax.psum(gen_part - data_part, "dp") - privacy_noise
    match_loss = lax.psum(jnp.sum(mean_gap * mean_gap), "feat") / (2.0 * total_feats)
    gap_rows = jnp.dot(
        gen_onehot, mean_gap.reshape(classes, 2 * feat_dev), precision=lax.Precision.HIGHEST
    ) * (16.0 * classes / total_gen)
    phase_grad = (
        jnp.cos(gen_phase) * gap_rows[:, feat_dev:] - jnp.sin(gen_phase) * gap_rows[:, :feat_dev]
    ).astype(jnp.bfloat16)
    partial_image = jnp.einsum(
        "gf,df->gd", phase_grad, frequencies, preferred_element_type=jnp.float32
    )
    image_grad = lax.psum(partial_image, "feat")
    grad_in, grad_out = generator_grads(
        image_grad, image_out, hidden, pre_hidden, sigmoid_h, latents, gen_out
    )
    grad_in, grad_out = (
        lax.psum_scatter(grad_in, "dp", scatter_dimension=0, tiled=True),
        lax.psum_scatter(grad_out, "dp", scatter_dimension=0, tiled=True),
    )
    return (match_loss, grad_in, grad_out)


def solution(mesh):
    return jax.shard_map(
        per_device,
        mesh=mesh,
        in_specs=(
            P("dp", None),
            P("dp"),
            P(None, "feat"),
            P(None, None, "feat"),
            P("dp", None),
            P("dp"),
            P(),
            P(),
        ),
        out_specs=(P(), P("dp", None), P("dp", None)),
        check_vma=False,
    )
```

profile of v0, /device:TPU:0, one launch (start us, length us, event | category | flops | bytes accessed | tf_op | source)
XLA Modules:
  0.0 356.0 jit_solution(9388458838005756762)
XLA Ops:
  7.2 0.0 copy-start
  7.2 0.0 all-reduce.3.cloned.1.call-start
  7.2 0.0 slice-start
  7.2 1.6 fusion.34
  8.8 1.0 copy-done.4
  9.8 4.8 %convolution_tanh_fusion = f32[256,3072]{1,0:T(8,128)S(1)} fusion(bf16[1024,3072]{1,0:T(8,128)(2,1)} %param.15, f32[256,1024]{1,0:T(8,128)S(1)} %fusion.34), kind=kOutput, calls=%fused_computation | convolution fusion | flops 1611923456 | bytes 10485760 | tf_op jit(solution)/shard_map/dot_general | solution.py:38
  14.6 5.3 %fusion.33 = (f32[256,1024]{1,0:T(8,128)S(1)}, f32[256,1024]{1,0:T(8,128)S(1)}) fusion(bf16[3072,1024]{1,0:T(8,128)(2,1)S(1)} %bitcast.19, f32[256,3072]{1,0:T(8,128)S(1)} %convolution_tanh_fusion), kind=kOutput, calls=%fused_computation.41 | convolution fusion | flops 1611399168 | bytes 11534336 | tf_op jit(solution)/shard_map/dot_general | solution.py:40
  20.0 0.0 copy-start.2
  20.0 0.0 copy-start.7
  20.0 12.3 %fusion.32 = (f32[384,1024]{1,0:T(8,128)S(1)}, f32[384,1024]{1,0:T(8,128)S(1)}) fusion(bf16[384,3072]{1,0:T(8,128)(2,1)S(1)} %copy-done, bf16[3072,1024]{1,0:T(8,128)(2,1)S(1)} %bitcast.19), kind=kOutput, calls=%fused_computation.40 | convolution fusion | flops 2415919104 | bytes 11796480 | tf_op jit(solution)/shard_map/dot_general | solution.py:33
  32.3 0.8 convolution_multiply_fusion.1
  33.1 1.2 fusion.7
  34.3 0.7 sub.22
  35.0 0.0 all-reduce.3.cloned.1.call-update
  35.0 0.2 all-reduce.5.cloned.1.call-start
  35.3 32.9 %all-reduce.3.cloned.1.call-done = f32[10,2,1024]{2,1,0:T(2,128)} async-done(((f32[10,2,1024]{2,1,0:T(2,128)}), f32[10,2,1024]{2,1,0:T(2,128)}) %all-reduce.3.cloned.1.call-update) | async-done | bytes 81936 | tf_op jit(solution)/shard_map/psum | solution.py:42
  68.2 1.7 multiply_reduce_fusion
  70.0 1.0 convolution_multiply_fusion
  71.0 6.4 %fusion.22 = f32[256,3072]{1,0:T(8,128)} fusion(bf16[3072,1024]{1,0:T(8,128)(2,1)} %param.10, f32[256,1024]{1,0:T(8,128)S(1)} %copy-done.3, f32[256,2048]{1,0:T(8,128)S(1)} %convolution_multiply_fusion, f32[256,1024]{1,0:T(8,128)S(1)} %get-tuple-element.13), kind=kOutput, calls=%fused_computation.28 | convolution fusion | flops 1611661312 | bytes 13631488 | tf_op jit(solution)/shard_map/gf,df->gd/dot_general | solution.py:50
  77.4 0.0 all-reduce.5.cloned.1.call-update
  77.5 0.0 reduce-scatter.7.cloned.1.call-start
  77.5 130.2 %all-reduce.5.cloned.1.call-done = f32[256,3072]{1,0:T(8,128)} async-done(((f32[256,3072]{1,0:T(8,128)}), f32[256,3072]{1,0:T(8,128)}) %all-reduce.5.cloned.1.call-update) | async-done | bytes 3145744 | tf_op jit(solution)/shard_map/psum | solution.py:53
  207.7 4.6 %multiply_convert_fusion = bf16[256,3072]{1,0:T(8,128)(2,1)} fusion(f32[256,3072]{1,0:T(8,128)} %all-reduce.5.cloned.1.call-done, f32[256,3072]{1,0:T(8,128)} %copy-done.1), kind=kLoop, calls=%fused_computation.5 | loop fusion | flops 3145728 | bytes 7864320 | tf_op jit(solution)/shard_map/convert_element_type | solution.py:15
  212.3 6.6 %convolution_bitcast_fusion = f32[256,1024]{0,1:T(8,128)} fusion(bf16[256,256]{1,0:T(8,128)(2,1)S(1)} %copy-done.6, bf16[256,3072]{1,0:T(8,128)(2,1)} %multiply_convert_fusion, bf16[1024,3072]{1,0:T(8,128)(2,1)} %param.15, f32[256,1024]{1,0:T(8,128)S(1)} %copy-done.5), kind=kOutput, calls=%fused_computation.17 | convolution fusion | flops 1747189760 | bytes 10092544 | tf_op jit(solution)/shard_map/gz,gh->zh/dot_general | solution.py:21
  218.9 2.6 copy.13
  221.5 0.0 reduce-scatter.7.cloned.1.call-update
  221.5 0.0 reduce-scatter.5.cloned.1.call-start
  221.5 8.0 %fusion.31 = f32[1024,3072]{1,0:T(8,128)} fusion(bf16[256,3072]{1,0:T(8,128)(2,1)} %multiply_convert_fusion, f32[256,1024]{1,0:T(8,128)S(1)} %copy-done.5), kind=kOutput, calls=%fused_computation.39 | convolution fusion | flops 1611923456 | bytes 15204352 | tf_op jit(solution)/shard_map/gh,gd->hd/dot_general | solution.py:16
  229.6 0.0 reduce-scatter.5.cloned.1.call-update
  229.6 19.9 %psum.22 = f32[]{:T(128)} all-reduce(f32[]{:T(128)} %get-tuple-element.9), channel_id=1, replica_groups=mesh['dp'=4,'feat'=8] {'feat'}, use_global_device_ids=true, to_apply=%region_2.0 | all-reduce | flops 1 | bytes 8 | tf_op jit(solution)/shard_map/psum | solution.py:43
  250.1 0.0 reduce-scatter.7.cloned.1.call-done
  250.1 98.3 %reduce-scatter.5.cloned.1.call-done = f32[256,3072]{1,0:T(8,128)} async-done(((f32[1024,3072]{1,0:T(8,128)}), f32[256,3072]{1,0:T(8,128)}) %reduce-scatter.5.cloned.1.call-update) | async-done | bytes 3145744 | tf_op jit(solution)/shard_map/reduce_scatter | solution.py:59
  (20 shorter events, 0.1 us)
Async XLA Ops:
  7.2 12.8 %copy-start = (bf16[384,3072]{1,0:T(8,128)(2,1)S(1)}, bf16[384,3072]{1,0:T(8,128)(2,1)}, u32[]{:S(2)}) copy-start(bf16[384,3072]{1,0:T(8,128)(2,1)} %param.8) | copy-start | bytes 7077892
  7.2 61.0 %all-reduce.3.cloned.1.call-start = ((), (), s32[]{:S(2)}) async-start(), calls=%async_computation.2 | async-start | bytes 163840 | tf_op jit(solution)/shard_map/psum | solution.py:42
  7.2 7.4 %slice-start = ((s8[6291456]{0:T(1024)(128)(4,1)}), s8[4194304]{0:T(1024)(128)(4,1)S(1)}, s32[]{:S(2)}) async-start(s8[6291456]{0:T(1024)(128)(4,1)} %bitcast.18), calls=%async_computation.6 | async-start | bytes 8388608
  8.8 1.0 copy-start.4
  9.8 4.8 %slice-start.1 = ((s8[6291456]{0:T(1024)(128)(4,1)}), s8[2097152]{0:T(1024)(128)(4,1)S(1)}, s32[]{:S(2)}) async-start(s8[6291456]{0:T(1024)(128)(4,1)} %bitcast.18), calls=%async_computation.7 | async-start | bytes 4194304
  14.6 5.3 %copy-start.1 = (f32[256,3072]{1,0:T(8,128)}, f32[256,3072]{1,0:T(8,128)S(1)}, u32[]{:S(2)}) copy-start(f32[256,3072]{1,0:T(8,128)S(1)} %convolution_tanh_fusion) | copy-start | bytes 9437188
  20.0 12.3 %copy-start.2 = (f32[256,1024]{1,0:T(8,128)}, f32[256,1024]{1,0:T(8,128)S(1)}, u32[]{:S(2)}) copy-start(f32[256,1024]{1,0:T(8,128)S(1)} %get-tuple-element.14) | copy-start | bytes 3145732
  20.0 12.3 %copy-start.7 = (s32[256]{0:T(256)S(1)}, s32[256]{0:T(256)}, u32[]{:S(2)}) copy-start(s32[256]{0:T(256)} %param.13) | copy-start | bytes 3076
  20.0 13.2 %copy-start.8 = (s32[384]{0:T(512)S(1)}, s32[384]{0:T(512)}, u32[]{:S(2)}) copy-start(s32[384]{0:T(512)} %param.9) | copy-start | bytes 4612
  35.0 172.7 %all-reduce.5.cloned.1.call-start = ((), (), s32[]{:S(2)}) async-start(), calls=%async_computation.3 | async-start | bytes 6291456 | tf_op jit(solution)/shard_map/psum | solution.py:53
  68.2 2.8 copy-start.3
  77.5 134.8 %copy-start.5 = (f32[256,1024]{1,0:T(8,128)S(1)}, f32[256,1024]{1,0:T(8,128)}, u32[]{:S(2)}) copy-start(f32[256,1024]{1,0:T(8,128)} %copy-done.4) | copy-start | bytes 3145732
  77.5 134.8 %copy-start.6 = (bf16[256,256]{1,0:T(8,128)(2,1)S(1)}, bf16[256,256]{1,0:T(8,128)(2,1)}, u32[]{:S(2)}) copy-start(bf16[256,256]{1,0:T(8,128)(2,1)} %param.12) | copy-start | bytes 393220
  77.5 172.6 %reduce-scatter.7.cloned.1.call-start = ((), (), s32[]{:S(2)}) async-start(), calls=%async_computation.5 | async-start | bytes 1310720
  221.5 126.9 %reduce-scatter.5.cloned.1.call-start = ((), (), s32[]{:S(2)}) async-start(), calls=%async_computation.4 | async-start | bytes 15728640 | tf_op jit(solution)/shard_map/reduce_scatter | solution.py:59
Sparse Core Ops, SparseCore 0:
  35.2 32.9 all-reduce.2
  77.6 130.0 all-reduce.4
  221.6 23.8 reduce-scatter.6
  248.5 99.8 reduce-scatter.4
where the time goes:
time: 356 us
  waiting for transfers between devices  261 us (73%)
  matrix products  47.9 us (13%)
  blocking collectives  19.9 us (6%)
  between operations  15.7 us (4%)
  other arithmetic  6.29 us (2%)
  local copies, waits for them, and re-layouts  4.46 us (1%)
    psum x1, waiting for transfers between devices, per_device(): image_grad = lax.psum(partial_image, 'feat')  130 us
    reduce_scatter x1, waiting for transfers between devices, per_device(): lax.psum_scatter(grad_out, 'dp', scatter_dimension=0, tiled=True)  98.3 us
    psum x1, waiting for transfers between devices, per_device(): mean_gap = lax.psum(gen_part - data_part, 'dp') - privacy_noise  32.9 us
    psum x1, blocking collectives, per_device(): lax.psum(jnp.sum(mean_gap * mean_gap), 'feat') / (2.0 * total_feats)  19.9 us
    dot_general x1, matrix products, per_device(): jnp.dot(images, frequencies, preferred_element_type=jnp.float32)  12.3 us
    dot_general x1, matrix products, generator_grads(): jnp.einsum('gh,gd->hd', hidden, out_grad, preferred_element_type=jnp.floa...  8.02 us
  transfers between devices with their start and end apart: 4, of which 3 were waited for; matrix products, arithmetic and copies ran while one was open for 2% of the time, Pallas kernels for 0%

commit v1 on v0

--- a/solution.py
+++ b/solution.py
@@ -50,7 +50,11 @@
     partial_image = jnp.einsum(
         "gf,df->gd", phase_grad, frequencies, preferred_element_type=jnp.float32
     )
-    image_grad = lax.psum(partial_image, "feat")
+    image_grad = partial_image
+    for hop in (1, 2, 4):
+        image_grad = image_grad + lax.ppermute(
+            image_grad, "feat", [(dev, dev ^ hop) for dev in range(8)]
+        )
     grad_in, grad_out = generator_grads(
         image_grad, image_out, hidden, pre_hidden, sigmoid_h, latents, gen_out
     )

time: 356 us -> 500 us (1.40)
  waiting for transfers between devices: 261 us -> 400 us
  starting transfers between devices: 0.35 us -> 6.38 us
    ppermute x0 -> x3, waiting for transfers between devices: none -> 270 us  [per_device(): lax.ppermute(image_grad, 'feat', [(dev, dev ^ hop) for dev in range(8)])]
    psum x1 -> x0, waiting for transfers between devices: 130 us -> none  [per_device(): image_grad = lax.psum(partial_image, 'feat')]
    ppermute x0 -> x3, starting transfers between devices: none -> 6.08 us  [per_device(): lax.ppermute(image_grad, 'feat', [(dev, dev ^ hop) for dev in range(8)])]
  transfers between devices with their start and end apart: 4 -> 6, of which waited for: 3 -> 5; matrix products, arithmetic and copies ran while one was open for 2% -> 2% of each run, Pallas kernels for 0% -> 0%
where the time goes in v1:
time: 500 us
  waiting for transfers between devices  400 us (80%)
  matrix products  46.2 us (9%)
  blocking collectives  22.2 us (4%)
  between operations  15.8 us (3%)
  starting transfers between devices  6.38 us (1%)
    ppermute x3, waiting for transfers between devices, per_device(): lax.ppermute(image_grad, 'feat', [(dev, dev ^ hop) for dev in range(8)])  270 us
    reduce_scatter x1, waiting for transfers between devices, per_device(): lax.psum_scatter(grad_out, 'dp', scatter_dimension=0, tiled=True)  97.1 us
    psum x1, waiting for transfers between devices, per_device(): mean_gap = lax.psum(gen_part - data_part, 'dp') - privacy_noise  32.9 us
    psum x1, blocking collectives, per_device(): lax.psum(jnp.sum(mean_gap * mean_gap), 'feat') / (2.0 * total_feats)  22.2 us
    dot_general x1, matrix products, per_device(): jnp.dot(images, frequencies, preferred_element_type=jnp.float32)  12.3 us
  transfers between devices with their start and end apart: 6, of which 5 were waited for; matrix products, arithmetic and copies ran while one was open for 2% of the time, Pallas kernels for 0%

profile of v1, /device:TPU:0, one launch (start us, length us, event | category | flops | bytes accessed | tf_op | source)
XLA Modules:
  0.0 499.8 jit_solution(3305933044144210588)
XLA Ops:
  7.2 0.0 all-reduce.2.cloned.1.call-start
  7.2 1.6 fusion.34
  8.8 1.0 copy-done.5
  9.8 4.8 convolution_tanh_fusion
  14.6 5.3 %fusion.33 = (f32[256,1024]{1,0:T(8,128)S(1)}, f32[256,1024]{1,0:T(8,128)S(1)}) fusion(bf16[3072,1024]{1,0:T(8,128)(2,1)S(1)} %bitcast.19, f32[256,3072]{1,0:T(8,128)S(1)} %convolution_tanh_fusion), kind=kOutput, calls=%fused_computation.41 | convolution fusion | flops 1611399168 | bytes 11534336 | tf_op jit(solution)/shard_map/dot_general | solution.py:40
  20.0 12.3 %fusion.32 = (f32[384,1024]{1,0:T(8,128)S(1)}, f32[384,1024]{1,0:T(8,128)S(1)}) fusion(bf16[384,3072]{1,0:T(8,128)(2,1)S(1)} %copy-done, bf16[3072,1024]{1,0:T(8,128)(2,1)S(1)} %bitcast.19), kind=kOutput, calls=%fused_computation.40 | convolution fusion | flops 2415919104 | bytes 11796480 | tf_op jit(solution)/shard_map/dot_general | solution.py:33
  32.3 0.8 convolution_multiply_fusion.1
  33.1 1.2 fusion.7
  34.3 0.7 sub.22
  35.0 0.0 all-reduce.2.cloned.1.call-update
  35.0 0.2 reduce-scatter.7.cloned.1.call-start
  35.2 32.9 %all-reduce.2.cloned.1.call-done = f32[10,2,1024]{2,1,0:T(2,128)} async-done(((f32[10,2,1024]{2,1,0:T(2,128)}), f32[10,2,1024]{2,1,0:T(2,128)}) %all-reduce.2.cloned.1.call-update) | async-done | bytes 81936 | tf_op jit(solution)/shard_map/psum | solution.py:42
  68.2 1.7 multiply_reduce_fusion
  70.0 1.0 convolution_multiply_fusion
  71.0 4.8 fusion.22
  75.8 1.5 collective-permute-start
  77.3 68.4 %collective-permute-done = f32[256,3072]{1,0:T(8,128)S(1)} collective-permute-done((f32[256,3072]{1,0:T(8,128)S(1)}, f32[256,3072]{1,0:T(8,128)S(1)}, u32[]{:S(2)}, u32[]{:S(2)}) %collective-permute-start) | collective-permute-done | bytes 3145760 | tf_op jit(solution)/shard_map/ppermute | solution.py:55
  145.7 0.5 add.24
  146.3 1.8 collective-permute-start.1
  148.1 67.6 %collective-permute-done.1 = f32[256,3072]{1,0:T(8,128)S(1)} collective-permute-done((f32[256,3072]{1,0:T(8,128)S(1)}, f32[256,3072]{1,0:T(8,128)S(1)}, u32[]{:S(2)}, u32[]{:S(2)}) %collective-permute-start.1) | collective-permute-done | bytes 3145760 | tf_op jit(solution)/shard_map/ppermute | solution.py:55
  215.7 0.4 add.25
  216.0 2.7 collective-permute-start.2
  218.8 134.1 %collective-permute-done.2 = f32[256,3072]{1,0:T(8,128)S(1)} collective-permute-done((f32[256,3072]{1,0:T(8,128)S(1)}, f32[256,3072]{1,0:T(8,128)S(1)}, u32[]{:S(2)}, u32[]{:S(2)}) %collective-permute-start.2) | collective-permute-done | bytes 3145760 | tf_op jit(solution)/shard_map/ppermute | solution.py:55
  352.9 2.1 multiply_convert_fusion
  355.0 6.6 %convolution_bitcast_fusion = f32[256,1024]{0,1:T(8,128)} fusion(bf16[256,256]{1,0:T(8,128)(2,1)S(1)} %copy-done.7, bf16[256,3072]{1,0:T(8,128)(2,1)} %multiply_convert_fusion, bf16[1024,3072]{1,0:T(8,128)(2,1)} %param.15, f32[256,1024]{1,0:T(8,128)S(1)} %copy-done.6), kind=kOutput, calls=%fused_computation.17 | convolution fusion | flops 1747189760 | bytes 10092544 | tf_op jit(solution)/shard_map/gz,gh->zh/dot_general | solution.py:21
  361.6 2.6 copy.13
  364.2 0.0 reduce-scatter.7.cloned.1.call-update
  364.2 0.0 reduce-scatter.5.cloned.1.call-start
  364.3 7.9 %fusion.31 = f32[1024,3072]{1,0:T(8,128)} fusion(bf16[256,3072]{1,0:T(8,128)(2,1)} %multiply_convert_fusion, f32[256,1024]{1,0:T(8,128)S(1)} %copy-done.6), kind=kOutput, calls=%fused_computation.39 | convolution fusion | flops 1611923456 | bytes 15204352 | tf_op jit(solution)/shard_map/gh,gd->hd/dot_general | solution.py:16
  372.3 22.2 %psum.15 = f32[]{:T(128)} all-reduce(f32[]{:T(128)} %get-tuple-element.9), channel_id=1, replica_groups=mesh['dp'=4,'feat'=8] {'feat'}, use_global_device_ids=true, to_apply=%region_2.0 | all-reduce | flops 1 | bytes 8 | tf_op jit(solution)/shard_map/psum | solution.py:43
  395.1 0.0 reduce-scatter.7.cloned.1.call-done
  395.1 97.1 %reduce-scatter.5.cloned.1.call-done = f32[256,3072]{1,0:T(8,128)} async-done(((f32[1024,3072]{1,0:T(8,128)}), f32[256,3072]{1,0:T(8,128)}) %reduce-scatter.5.cloned.1.call-update) | async-done | bytes 3145744 | tf_op jit(solution)/shard_map/reduce_scatter | solution.py:63
  (27 shorter events, 0.2 us)
Async XLA Ops:
  7.2 12.8 %copy-start = (bf16[384,3072]{1,0:T(8,128)(2,1)S(1)}, bf16[384,3072]{1,0:T(8,128)(2,1)}, u32[]{:S(2)}) copy-start(bf16[384,3072]{1,0:T(8,128)(2,1)} %param.8) | copy-start | bytes 7077892
  7.2 61.0 %all-reduce.2.cloned.1.call-start = ((), (), s32[]{:S(2)}) async-start(), calls=%async_computation.2 | async-start | bytes 163840 | tf_op jit(solution)/shard_map/psum | solution.py:42
  7.2 7.3 %slice-start = ((s8[6291456]{0:T(1024)(128)(4,1)}), s8[4194304]{0:T(1024)(128)(4,1)S(1)}, s32[]{:S(2)}) async-start(s8[6291456]{0:T(1024)(128)(4,1)} %bitcast.18), calls=%async_computation.5 | async-start | bytes 8388608
  8.8 1.0 copy-start.5
  9.8 4.8 slice-start.1
  14.6 5.3 %copy-start.1 = (f32[256,3072]{1,0:T(8,128)}, f32[256,3072]{1,0:T(8,128)S(1)}, u32[]{:S(2)}) copy-start(f32[256,3072]{1,0:T(8,128)S(1)} %convolution_tanh_fusion) | copy-start | bytes 9437188
  19.9 12.3 %copy-start.3 = (f32[256,1024]{1,0:T(8,128)}, f32[256,1024]{1,0:T(8,128)S(1)}, u32[]{:S(2)}) copy-start(f32[256,1024]{1,0:T(8,128)S(1)} %get-tuple-element.14) | copy-start | bytes 3145732
  19.9 12.3 %copy-start.8 = (s32[256]{0:T(256)S(1)}, s32[256]{0:T(256)}, u32[]{:S(2)}) copy-start(s32[256]{0:T(256)} %param.13) | copy-start | bytes 3076
  20.0 13.1 %copy-start.9 = (s32[384]{0:T(512)S(1)}, s32[384]{0:T(512)}, u32[]{:S(2)}) copy-start(s32[384]{0:T(512)} %param.9) | copy-start | bytes 4612
  35.0 360.1 %reduce-scatter.7.cloned.1.call-start = ((), (), s32[]{:S(2)}) async-start(), calls=%async_computation.4 | async-start | bytes 1310720
  68.2 2.8 copy-start.4
  75.8 70.0 %collective-permute-start = (f32[256,3072]{1,0:T(8,128)S(1)}, f32[256,3072]{1,0:T(8,128)S(1)}, u32[]{:S(2)}, u32[]{:S(2)}) collective-permute-start(f32[256,3072]{1,0:T(8,128)S(1)} %fusion.22), channel_id=1, source_target_pairs={{0,1},{1,0},{2,3},{3,2},{4,5},{5,4},{6,7},{7,6},{8,9},{9,8},{10,11... | collective-permute-start | bytes 9437192 | tf_op jit(solution)/shard_map/ppermute | solution.py:55
  146.2 206.7 %copy-start.2 = (f32[256,3072]{1,0:T(8,128)S(1)}, f32[256,3072]{1,0:T(8,128)}, u32[]{:S(2)}) copy-start(f32[256,3072]{1,0:T(8,128)} %copy-done.1) | copy-start | bytes 9437188
  146.3 69.4 %collective-permute-start.1 = (f32[256,3072]{1,0:T(8,128)S(1)}, f32[256,3072]{1,0:T(8,128)S(1)}, u32[]{:S(2)}, u32[]{:S(2)}) collective-permute-start(f32[256,3072]{1,0:T(8,128)S(1)} %add.24), channel_id=1, source_target_pairs={{0,2},{1,3},{2,0},{3,1},{4,6},{5,7},{6,4},{7,5},{8,10},{9,11},{10,... | collective-permute-start | bytes 9437192 | tf_op jit(solution)/shard_map/ppermute | solution.py:55
  216.0 139.0 %copy-start.6 = (f32[256,1024]{1,0:T(8,128)S(1)}, f32[256,1024]{1,0:T(8,128)}, u32[]{:S(2)}) copy-start(f32[256,1024]{1,0:T(8,128)} %copy-done.5) | copy-start | bytes 3145732
  216.0 139.0 %copy-start.7 = (bf16[256,256]{1,0:T(8,128)(2,1)S(1)}, bf16[256,256]{1,0:T(8,128)(2,1)}, u32[]{:S(2)}) copy-start(bf16[256,256]{1,0:T(8,128)(2,1)} %param.12) | copy-start | bytes 393220
  216.0 136.9 %collective-permute-start.2 = (f32[256,3072]{1,0:T(8,128)S(1)}, f32[256,3072]{1,0:T(8,128)S(1)}, u32[]{:S(2)}, u32[]{:S(2)}) collective-permute-start(f32[256,3072]{1,0:T(8,128)S(1)} %add.25), channel_id=1, source_target_pairs={{0,4},{1,5},{2,6},{3,7},{4,0},{5,1},{6,2},{7,3},{8,12},{9,13},{10,... | collective-permute-start | bytes 9437192 | tf_op jit(solution)/shard_map/ppermute | solution.py:55
  364.2 127.9 %reduce-scatter.5.cloned.1.call-start = ((), (), s32[]{:S(2)}) async-start(), calls=%async_computation.3 | async-start | bytes 15728640 | tf_op jit(solution)/shard_map/reduce_scatter | solution.py:63
Sparse Core Ops, SparseCore 0:
  35.1 32.9 all-reduce.1
  364.4 24.9 reduce-scatter.6
  392.5 99.6 reduce-scatter.4
